TPU v7x, 32 devices: a whole 2x2x4 slice. The times are simulated.
32 devices in a mesh: batch: 4 (over x, core), hidden: 4 (over z), solver: 2 (over y).
Axes of the slice: x: 2, y: 2, z: 4, core: 2. Of those that a mesh axis runs over, the one named last changes fastest.
Arguments:
- activations: bfloat16 [1024, 4096], P('batch', ('hidden', 'solver')), may hold values from -16 to 16, as said below
- cotangent: bfloat16 [8192, 1024], P(('hidden', 'solver'), 'batch'), may hold values from -0.1875 to 0.1875
- weight: bfloat16 [4096, 8192], P(('hidden', 'solver'), 'batch'), may hold values from -0.09375 to 0.09375
- left_old: float32 [4, 8, 1024, 1024], P('hidden', 'batch'), may hold values from -0.001953125 to 2.0019531, as said below
- right_old: float32 [4, 8, 1024, 1024], P('hidden', 'batch'), may hold values from -0.001953125 to 2.0019531, as said below
Outputs:
- first_out: bfloat16 [8192, 1024], P(('hidden', 'solver'), 'batch')
- new_left: float32 [4, 8, 1024, 1024], P('hidden', 'batch', 'solver')
- new_right: float32 [4, 8, 1024, 1024], P('hidden', 'batch', 'solver')
- direction: float32 [4096, 8192], P(('hidden', 'solver'), 'batch')
- second_out: bfloat16 [8192, 1024], P(('hidden', 'solver'), 'batch')
Inputs may be any that keep to these rules, and one draw needn't show every extreme that they name: `activations`: in the hidden draw each feature carries its own scale. `left_old`: every block is symmetric, its diagonal is positive and larger than the sum of the magnitudes of the rest of its row. `right_old`: every block is symmetric, its diagonal is positive and larger than the sum of the magnitudes of the rest of its row.
All inputs are finite; a program needn't handle non-finite values. Where the computation divides by a largest or mean magnitude, that divisor is 1e-20 or more.
Results may differ from a plain program's by a relative error of at most 0.017.
Values may be sent and summed in bfloat16 or wider, within the bound.
A program may use at most 128 MiB of HBM per device.

v0:
```python
import jax
import jax.numpy as jnp
from jax import lax
from jax.sharding import PartitionSpec as P

BLOCK = 1024
STAT_DECAY = 0.8
LEARN_RATE = 0.005
EPSILON = 1e-06


def product(left_mat, right_mat):
    return jnp.einsum(
        "bij,bjk->bik",
        left_mat,
        right_mat,
        precision=lax.Precision.HIGHEST,
        preferred_element_type=jnp.float32,
    )


def prepare(factor):
    identity = jnp.eye(BLOCK, dtype=jnp.float32)
    scaled = 2.5 / (jnp.max(jnp.sum(jnp.abs(factor), axis=2), axis=1) + EPSILON)
    moment = scaled[:, None, None] * factor
    newton_step = (5.0 * identity - moment) * 0.25
    return (scaled, moment, newton_step)


def transposed_product(weight_cols, acts):
    return lax.dot_general(
        weight_cols, acts, (((0,), (1,)), ((), ())), preferred_element_type=jnp.float32
    )


def body(activations, cotangent, weight, left_old, right_old):
    rows_here = weight.shape[0]
    nblocks = weight.shape[1] // BLOCK
    weight_rows = lax.all_gather(weight, "batch", axis=1, tiled=True)
    columns = weight_rows
    first_sum = lax.psum_scatter(
        transposed_product(columns, activations).astype(jnp.bfloat16),
        ("hidden", "solver"),
        scatter_dimension=0,
        tiled=True,
    )
    cotangent_all = lax.all_gather(cotangent, ("hidden", "solver"), axis=0, tiled=True)
    grad_local = lax.psum_scatter(
        jnp.dot(cotangent_all, activations, preferred_element_type=jnp.float32).astype(
            jnp.bfloat16
        ),
        "batch",
        scatter_dimension=0,
        tiled=True,
    )
    grad_blocks = grad_local.reshape(nblocks, BLOCK, rows_here)
    grad_full = lax.all_gather(grad_blocks, "solver", axis=2, tiled=True)
    gram_left = jnp.einsum("bnm,bnk->bmk", grad_full, grad_full, preferred_element_type=jnp.float32)
    gram_right = jnp.einsum(
        "bnm,bkm->bnk", grad_full, grad_full, preferred_element_type=jnp.float32
    )
    left_all = STAT_DECAY * left_old[0] + (1.0 - STAT_DECAY) / BLOCK * gram_left
    right_all = STAT_DECAY * right_old[0] + (1.0 - STAT_DECAY) / BLOCK * gram_right
    first_row = lax.axis_index("solver") * rows_here
    new_left = lax.dynamic_slice_in_dim(left_all, first_row, rows_here, 1)[None]
    new_right = lax.dynamic_slice_in_dim(right_all, first_row, rows_here, 1)[None]
    scale_left, moment_left, step_left = prepare(left_all)
    own_rows = lax.dynamic_slice_in_dim(step_left, first_row, rows_here, 1)
    power_rows = product(
        product(product(product(own_rows, step_left), step_left), step_left), moment_left
    )
    row_index = lax.broadcasted_iota(jnp.int32, (rows_here, BLOCK), 0) + first_row
    col_index = lax.broadcasted_iota(jnp.int32, (rows_here, BLOCK), 1)
    eye_rows = (row_index == col_index).astype(jnp.float32)
    next_rows = (5.0 * eye_rows - power_rows) * 0.25
    root_rows = (scale_left**0.25)[:, None, None] * product(next_rows, step_left)
    grad_float = grad_full.astype(jnp.float32)
    mixed_rows = jnp.einsum(
        "brm,bnm->brn",
        root_rows,
        grad_float,
        precision=lax.Precision.HIGHEST,
        preferred_element_type=jnp.float32,
    )
    scale_right, moment_right, step_right = prepare(right_all)
    turned = product(mixed_rows, step_right)
    power_right = product(
        product(product(product(product(turned, step_right), step_right), step_right), step_right),
        moment_right,
    )
    update = (scale_right**0.25)[:, None, None] * ((5.0 * turned - power_right) * 0.25)
    squares = lax.psum(jnp.sum(update * update, axis=(1, 2)), "solver")
    spread = jnp.sqrt(squares / (BLOCK * BLOCK) + EPSILON)
    scaled_update = update / spread[:, None, None]
    direction = jnp.transpose(scaled_update, (1, 0, 2)).reshape(rows_here, nblocks * BLOCK)
    new_weight = (weight.astype(jnp.float32) - LEARN_RATE * direction).astype(jnp.bfloat16)
    new_rows = lax.all_gather(new_weight, "batch", axis=1, tiled=True)
    columns = new_rows
    second_sum = lax.psum_scatter(
        transposed_product(columns, activations).astype(jnp.bfloat16),
        ("hidden", "solver"),
        scatter_dimension=0,
        tiled=True,
    )
    return (first_sum, new_left, new_right, direction, second_sum)


def solution(mesh):
    in_specs = (
        P("batch", ("hidden", "solver")),
        P(("hidden", "solver"), "batch"),
        P(("hidden", "solver"), "batch"),
        P("hidden", "batch", None, None),
        P("hidden", "batch", None, None),
    )
    out_specs = (
        P(("hidden", "solver"), "batch"),
        P("hidden", "batch", "solver", None),
        P("hidden", "batch", "solver", None),
        P(("hidden", "solver"), "batch"),
        P(("hidden", "solver"), "batch"),
    )
    return jax.shard_map(body, mesh=mesh, in_specs=in_specs, out_specs=out_specs, check_vma=False)
```

profile of v0, /device:TPU:0, one launch (start us, length us, event | category | flops | bytes accessed | tf_op | source)
XLA Modules:
  0.0 721.3 jit_solution(6583412201741329409)
XLA Ops:
  7.2 0.0 copy-start
  7.2 0.0 all-gather.7.cloned.1.call-start
  7.2 0.7 all-gather.7.cloned.1.call-update
  7.9 0.0 reduce-scatter.6.cloned.1.call-start
  8.0 77.7 %all-gather.7.cloned.1.call-done = bf16[8192,256]{1,0:T(8,128)(2,1)} async-done(((bf16[1024,256]{1,0:T(8,128)(2,1)}), bf16[8192,256]{1,0:T(8,128)(2,1)}) %all-gather.7.cloned.1.call-update) | async-done | bytes 4194320 | tf_op jit(solution)/shard_map/all_gather | solution.py:47
  85.7 0.0 copy-done
  85.7 7.8 %convolution_convert_fusion = bf16[8192,512]{1,0:T(8,128)(2,1)} fusion(bf16[8192,256]{1,0:T(8,128)(2,1)} %all-gather.7.cloned.1.call-done, bf16[256,512]{1,0:T(8,128)(2,1)S(1)} %copy-done), kind=kOutput, calls=%fused_computation | convolution fusion | flops 2151677952 | bytes 12845056 | tf_op jit(solution)/shard_map/dot_general | solution.py:49
  93.4 0.0 reduce-scatter.6.cloned.1.call-update
  93.5 0.0 all-gather.9.cloned.1.call-start
  93.5 70.0 %reduce-scatter.6.cloned.1.call-done = bf16[2048,512]{1,0:T(8,128)(2,1)} async-done(((bf16[8192,512]{1,0:T(8,128)(2,1)}), bf16[2048,512]{1,0:T(8,128)(2,1)}) %reduce-scatter.6.cloned.1.call-update) | async-done | bytes 2097168 | tf_op jit(solution)/shard_map/reduce_scatter | solution.py:48
  163.5 3.9 copy.32
  167.4 0.0 all-gather.9.cloned.1.call-update
  167.5 0.0 all-gather.5.cloned.1.call-start
  167.5 0.5 all-gather.5.cloned.1.call-update
  168.0 0.2 all-gather.11.cloned.1.call-start
  168.3 2.5 fusion.13
  170.8 0.0 copy-done.2
  170.8 2.5 copy.53
  173.3 9.1 %copy.31 = f32[1,2,1024,1024]{2,3,1,0:T(8,128)} copy(f32[1,2,1024,1024]{3,2,1,0:T(8,128)} %param.8) | data formatting | bytes 16777216 | tf_op args[3]
  182.4 8.7 %copy.35 = f32[1,2,1024,1024]{2,3,1,0:T(8,128)} copy(f32[1,2,1024,1024]{3,2,1,0:T(8,128)} %param.9) | data formatting | bytes 16777216 | tf_op args[4]
  191.1 0.2 fusion.17
  191.3 33.1 %all-gather.9.cloned.1.call-done = bf16[2,1024,1024]{1,2,0:T(8,128)(2,1)} async-done(((bf16[2,1024,512]{1,2,0:T(8,128)(2,1)}), bf16[2,1024,1024]{1,2,0:T(8,128)(2,1)}) %all-gather.9.cloned.1.call-update) | async-done | bytes 4194320 | tf_op jit(solution)/shard_map/all_gather | solution.py:57
  224.4 15.2 %abs_reduce_fusion.1 = (f32[2,1024]{1,0:T(2,128)S(1)}, f32[2,1024,1024]{1,2,0:T(8,128)}) fusion(bf16[2,1024,1024]{1,2,0:T(8,128)(2,1)} %all-gather.9.cloned.1.call-done, f32[1,2,1024,1024]{2,3,1,0:T(8,128)} %copy.31), kind=kOutput, calls=%fused_computation.8 | convolution fusion | flops 4305451008 | bytes 20979712 | tf_op jit(solution)/shard_map/bnm,bnk->bmk/dot_general | solution.py:58
  239.6 0.0 copy-done.4
  239.6 10.1 %abs_reduce_fusion = (f32[2,1024]{1,0:T(2,128)S(1)}, f32[2,1024,1024]{1,2,0:T(8,128)}) fusion(bf16[2,1024,1024]{1,2,0:T(8,128)(2,1)S(1)} %copy-done.4, f32[1,2,1024,1024]{2,3,1,0:T(8,128)} %copy.35), kind=kOutput, calls=%fused_computation.6 | convolution fusion | flops 4305451008 | bytes 20979712 | tf_op jit(solution)/shard_map/bnm,bkm->bnk/dot_general | solution.py:59
  249.7 0.1 reduce_max.18
  249.8 0.1 reduce_max.19
  250.0 11.5 %subtract_multiply_fusion = (f32[2,1024,1024]{1,2,0:T(8,128)S(1)}, f32[2,1024,1024]{1,2,0:T(8,128)}) fusion(f32[2,1024,1024]{1,2,0:T(8,128)} %get-tuple-element.22, f32[2]{0:T(128)S(1)} %get-tuple-element.16, f32[1024,1024]{0,1:T(8,128)} %fusion.13, f32[2,1024,1024]{1,2,0:T(8,128)} %get-tuple-element.24, f32[2]{0:T(128)S(1)} %get-tuple-element.28), kind=kLoop, calls=%fused_computation.5 | loop fusion | flops 12582912 | bytes 37748752 | tf_op jit(solution)/shard_map/mul | solution.py:26
  261.4 31.4 %fusion.10 = f32[2,512,1024]{2,1,0:T(8,128)S(1)} fusion(f32[2,1024,1024]{1,2,0:T(8,128)} %get-tuple-element.20, s32[]{:T(128)S(6)} %select_n.2), kind=kOutput, calls=%fused_computation.23 | convolution fusion | flops 12884901888 | bytes 16777220 | tf_op jit(solution)/shard_map/bij,bjk->bik/dot_general | solution.py:13
  292.9 0.0 copy-done.1
  292.9 14.3 %fusion.22 = f32[2,512,1024]{2,1,0:T(8,128)S(1)} fusion(f32[2,512,1024]{2,1,0:T(8,128)S(1)} %fusion.10, f32[2,1024,1024]{1,2,0:T(8,128)S(1)} %copy-done.1), kind=kOutput, calls=%fused_computation.43 | convolution fusion | flops 12884901888 | bytes 16777216 | tf_op jit(solution)/shard_map/bij,bjk->bik/dot_general | solution.py:13
  307.1 14.3 %fusion.23 = f32[2,512,1024]{2,1,0:T(8,128)S(1)} fusion(f32[2,512,1024]{2,1,0:T(8,128)S(1)} %fusion.22, f32[2,1024,1024]{1,2,0:T(8,128)S(1)} %copy-done.1), kind=kOutput, calls=%fused_computation.44 | convolution fusion | flops 12884901888 | bytes 16777216 | tf_op jit(solution)/shard_map/bij,bjk->bik/dot_general | solution.py:13
  321.5 16.3 %fusion.2 = f32[2,512,1024]{2,1,0:T(8,128)S(1)} fusion(f32[2,512,1024]{2,1,0:T(8,128)S(1)} %fusion.23, f32[2,1024,1024]{1,2,0:T(8,128)} %get-tuple-element.24, f32[2]{0:T(128)S(1)} %get-tuple-element.28), kind=kOutput, calls=%fused_computation.11 | convolution fusion | flops 12886999040 | bytes 16777224 | tf_op jit(solution)/shard_map/bij,bjk->bik/dot_general | solution.py:13
  337.8 15.6 %fusion.7 = f32[2,512,1024]{2,1,0:T(8,128)} fusion(f32[2,1024,1024]{1,2,0:T(8,128)S(1)} %copy-done.1, f32[2,512,1024]{2,1,0:T(8,128)S(1)} %fusion.2, f32[512,1024]{1,0:T(8,128)S(1)} %fusion.17), kind=kOutput, calls=%fused_computation.20 | convolution fusion | flops 12886999040 | bytes 18874368 | tf_op jit(solution)/shard_map/bij,bjk->bik/dot_general | solution.py:13
  353.4 9.4 %fusion.5 = f32[2,512,1024]{2,1,0:T(8,128)S(1)} fusion(bf16[2,1024,1024]{1,2,0:T(8,128)(2,1)} %all-gather.9.cloned.1.call-done, f32[2,512,1024]{2,1,0:T(8,128)} %fusion.7, f32[2]{0:T(128)S(1)} %get-tuple-element.27), kind=kOutput, calls=%fused_computation.18 | convolution fusion | flops 12885950464 | bytes 12582920 | tf_op jit(solution)/shard_map/brm,bnm->brn/dot_general | solution.py:78
  362.8 14.3 %fusion.24 = f32[2,512,1024]{2,1,0:T(8,128)S(1)} fusion(f32[2,512,1024]{2,1,0:T(8,128)S(1)} %fusion.5, f32[2,1024,1024]{1,2,0:T(8,128)S(1)} %get-tuple-element.19), kind=kOutput, calls=%fused_computation.45 | convolution fusion | flops 12884901888 | bytes 16777216 | tf_op jit(solution)/shard_map/bij,bjk->bik/dot_general | solution.py:13
  377.2 14.6 %fusion.25 = f32[2,512,1024]{2,1,0:T(8,128)S(1)} fusion(f32[2,512,1024]{2,1,0:T(8,128)S(1)} %fusion.24, f32[2,1024,1024]{1,2,0:T(8,128)S(1)} %get-tuple-element.19), kind=kOutput, calls=%fused_computation.46 | convolution fusion | flops 12884901888 | bytes 16777216 | tf_op jit(solution)/shard_map/bij,bjk->bik/dot_general | solution.py:13
  391.7 14.3 %fusion.26 = f32[2,512,1024]{2,1,0:T(8,128)S(1)} fusion(f32[2,512,1024]{2,1,0:T(8,128)S(1)} %fusion.25, f32[2,1024,1024]{1,2,0:T(8,128)S(1)} %get-tuple-element.19), kind=kOutput, calls=%fused_computation.47 | convolution fusion | flops 12884901888 | bytes 16777216 | tf_op jit(solution)/shard_map/bij,bjk->bik/dot_general | solution.py:13
  406.0 0.0 slice-start
  406.0 14.4 %fusion.27 = f32[2,512,1024]{2,1,0:T(8,128)S(1)} fusion(f32[2,512,1024]{2,1,0:T(8,128)S(1)} %fusion.26, f32[2,1024,1024]{1,2,0:T(8,128)S(1)} %get-tuple-element.19), kind=kOutput, calls=%fused_computation.48 | convolution fusion | flops 12884901888 | bytes 16777216 | tf_op jit(solution)/shard_map/bij,bjk->bik/dot_general | solution.py:13
  420.4 0.0 slice-start.1
  420.4 14.7 %fusion.28 = f32[2,512,1024]{2,1,0:T(8,128)S(1)} fusion(f32[2,512,1024]{2,1,0:T(8,128)S(1)} %fusion.27, f32[2,1024,1024]{1,2,0:T(8,128)S(1)} %get-tuple-element.19), kind=kOutput, calls=%fused_computation.49 | convolution fusion | flops 12884901888 | bytes 16777216 | tf_op jit(solution)/shard_map/bij,bjk->bik/dot_general | solution.py:13
  435.1 0.0 slice-done
  435.2 16.0 %multiply_reduce_fusion = (f32[2]{0:T(128)S(1)}, f32[2,512,1024]{2,1,0:T(8,128)}) fusion(f32[2]{0:T(128)S(1)} %get-tuple-element.15, f32[2,512,1024]{2,1,0:T(8,128)S(1)} %fusion.28, f32[2,1024,1024]{1,2,0:T(8,128)S(1)} %bitcast.41, f32[2]{0:T(128)S(1)} %get-tuple-element.16, f32[2,512,1024]{2,1,0:T(8,128)S(1)} %fusion.24), kind=kOutput, calls=%fused_computation.15 | convolution fusion | flops 12892241920 | bytes 20971544 | tf_op jit(solution)/shard_map/bij,bjk->bik/dot_general | solution.py:13
  451.2 4.9 psum.7
  456.1 5.1 divide_bitcast_fusion
  461.2 5.5 copy.52
  466.7 4.2 subtract_convert_fusion
  470.9 0.0 all-gather.11.cloned.1.call-update
  471.0 0.0 reduce-scatter.4.cloned.1.call-start
  471.0 0.0 all-gather.5.cloned.1.call-done
  471.0 7.9 %convolution_convert_fusion.2 = bf16[8192,256]{1,0:T(8,128)(2,1)} fusion(bf16[512,8192]{1,0:T(8,128)(2,1)} %all-gather.5.cloned.1.call-done, bf16[256,512]{1,0:T(8,128)(2,1)S(1)} %copy-done), kind=kOutput, calls=%fused_computation.2 | convolution fusion | flops 2149580800 | bytes 12845056 | tf_op jit(solution)/shard_map/dot_general | solution.py:31
  478.9 0.0 reduce-scatter.4.cloned.1.call-update
  478.9 0.3 reduce-scatter.8.cloned.1.call-start
  479.2 50.5 %all-gather.11.cloned.1.call-done = bf16[512,8192]{0,1:T(8,128)(2,1)} async-done(((bf16[512,2048]{0,1:T(8,128)(2,1)}), bf16[512,8192]{0,1:T(8,128)(2,1)}) %all-gather.11.cloned.1.call-update) | async-done | bytes 8388624 | tf_op jit(solution)/shard_map/all_gather | solution.py:97
  529.7 7.7 %convolution_convert_fusion.1 = bf16[8192,256]{1,0:T(8,128)(2,1)} fusion(bf16[512,8192]{0,1:T(8,128)(2,1)} %all-gather.11.cloned.1.call-done, bf16[256,512]{1,0:T(8,128)(2,1)S(1)} %copy-done), kind=kOutput, calls=%fused_computation.1 | convolution fusion | flops 2149580800 | bytes 12845056 | tf_op jit(solution)/shard_map/dot_general | solution.py:31
  537.4 0.0 reduce-scatter.8.cloned.1.call-update
  537.4 5.4 copy.54
  542.8 4.6 constant_dynamic-slice_fusion.1
  547.4 5.4 copy.34
  552.8 4.6 constant_dynamic-slice_fusion
  557.5 5.5 copy.38
  562.9 59.1 %reduce-scatter.4.cloned.1.call-done = bf16[1024,256]{1,0:T(8,128)(2,1)} async-done(((bf16[8192,256]{1,0:T(8,128)(2,1)}), bf16[1024,256]{1,0:T(8,128)(2,1)}) %reduce-scatter.4.cloned.1.call-update) | async-done | bytes 524304 | tf_op jit(solution)/shard_map/reduce_scatter | solution.py:41
  622.1 92.1 %reduce-scatter.8.cloned.1.call-done = bf16[1024,256]{1,0:T(8,128)(2,1)} async-done(((bf16[8192,256]{1,0:T(8,128)(2,1)}), bf16[1024,256]{1,0:T(8,128)(2,1)}) %reduce-scatter.8.cloned.1.call-update) | async-done | bytes 524304 | tf_op jit(solution)/shard_map/reduce_scatter | solution.py:99
  (10 shorter events, 0.0 us)
Async XLA Ops:
  7.2 78.5 %copy-start = (bf16[256,512]{1,0:T(8,128)(2,1)S(1)}, bf16[256,512]{1,0:T(8,128)(2,1)}, u32[]{:S(2)}) copy-start(bf16[256,512]{1,0:T(8,128)(2,1)} %param.5) | copy-start | bytes 786436
  7.2 78.5 %all-gather.7.cloned.1.call-start = ((), (), s32[]{:S(2)}) async-start(), calls=%async_computation.5 | async-start | bytes 4718592 | tf_op jit(solution)/shard_map/all_gather | solution.py:47
  7.9 155.6 %reduce-scatter.6.cloned.1.call-start = ((), (), s32[]{:S(2)}) async-start(), calls=%async_computation.6 | async-start | bytes 10485760 | tf_op jit(solution)/shard_map/reduce_scatter | solution.py:48
  93.5 130.9 %all-gather.9.cloned.1.call-start = ((), (), s32[]{:S(2)}) async-start(), calls=%async_computation.7 | async-start | bytes 6291456 | tf_op jit(solution)/shard_map/all_gather | solution.py:57
  167.4 3.4 copy-start.2
  167.5 303.6 %all-gather.5.cloned.1.call-start = ((), (), s32[]{:S(2)}) async-start(), calls=%async_computation.3 | async-start | bytes 10485760 | tf_op jit(solution)/shard_map/all_gather | solution.py:39
  168.0 361.7 %all-gather.11.cloned.1.call-start = ((), (), s32[]{:S(2)}) async-start(), calls=%async_computation.8 | async-start | bytes 10485760 | tf_op jit(solution)/shard_map/all_gather | solution.py:97
  224.4 15.2 %copy-start.4 = (bf16[2,1024,1024]{1,2,0:T(8,128)(2,1)S(1)}, bf16[2,1024,1024]{1,2,0:T(8,128)(2,1)}, u32[]{:S(2)}) copy-start(bf16[2,1024,1024]{1,2,0:T(8,128)(2,1)} %all-gather.9.cloned.1.call-done) | copy-start | bytes 12582916
  261.4 31.5 %copy-start.1 = (f32[2,1024,1024]{1,2,0:T(8,128)S(1)}, f32[2,1024,1024]{1,2,0:T(8,128)}, u32[]{:S(2)}) copy-start(f32[2,1024,1024]{1,2,0:T(8,128)} %get-tuple-element.20) | copy-start | bytes 25165828
  406.0 29.1 %slice-start = ((s8[8388608]{0:T(1024)(128)(4,1)}), s8[4194304]{0:T(1024)(128)(4,1)S(1)}, s32[]{:S(2)}) async-start(s8[8388608]{0:T(1024)(128)(4,1)} %bitcast.40), calls=%async_computation.10 | async-start | bytes 8388608
  420.4 14.7 %slice-start.1 = ((s8[8388608]{0:T(1024)(128)(4,1)}), s8[4194304]{0:T(1024)(128)(4,1)S(1)}, s32[]{:S(2)}) async-start(s8[8388608]{0:T(1024)(128)(4,1)} %bitcast.40), calls=%async_computation.11 | async-start | bytes 8388608
  461.2 5.5 copy-start.3
  471.0 151.1 %reduce-scatter.4.cloned.1.call-start = ((), (), s32[]{:S(2)}) async-start(), calls=%async_computation.4 | async-start | bytes 4718592 | tf_op jit(solution)/shard_map/reduce_scatter | solution.py:41
  478.9 235.3 %reduce-scatter.8.cloned.1.call-start = ((), (), s32[]{:S(2)}) async-start(), calls=%async_computation.9 | async-start | bytes 4718592 | tf_op jit(solution)/shard_map/reduce_scatter | solution.py:99
Sparse Core Ops, SparseCore 0:
  10.1 75.5 all-gather.6
  93.6 69.8 reduce-scatter.5
  167.6 56.7 all-gather.8
  225.8 58.2 all-gather.4
  471.1 58.5 all-gather.10
  533.8 88.2 reduce-scatter.3
  626.3 87.8 reduce-scatter.7
where the time goes:
time: 725 us; the launch traced here: 721 us
  waiting for transfers between devices  384 us (53%)
  matrix products  238 us (33%)
  local copies, waits for them, and re-layouts  55.2 us (8%)
  other arithmetic  23.8 us (3%)
  between operations  14.5 us (2%)
    dot_general x11, matrix products, product(): jnp.einsum('bij,bjk->bik', left_mat, right_mat, precision=lax.Precision.H...  180 us
    reduce_scatter x2, waiting for transfers between devices, body(): lax.psum_scatter(transposed_product(columns, activations).astype(jnp.bflo...  151 us
    all_gather x1, waiting for transfers between devices, body(): lax.all_gather(cotangent, ('hidden', 'solver'), axis=0, tiled=True)  77.7 us
    reduce_scatter x1, waiting for transfers between devices, body(): lax.psum_scatter(jnp.dot(cotangent_all, activations, preferred_element_ty...  70 us
    all_gather x1, waiting for transfers between devices, body(): new_rows = lax.all_gather(new_weight, 'batch', axis=1, tiled=True)  50.5 us
    all_gather x1, waiting for transfers between devices, body(): grad_full = lax.all_gather(grad_blocks, 'solver', axis=2, tiled=True)  33.1 us
    unnamed x18, local copies, waits for them, and re-layouts  25.7 us
    dot_general x2, matrix products, transposed_product(): lax.dot_general(weight_cols, acts, (((0,), (1,)), ((), ())), preferred_el...  15.6 us
  transfers between devices with their start and end apart: 7, of which 6 were waited for; matrix products, arithmetic and copies ran while one was open for 42% of the time, Pallas kernels for 0%

commit v1 on v0

--- a/solution.py
+++ b/solution.py
@@ -94,7 +94,14 @@
     scaled_update = update / spread[:, None, None]
     direction = jnp.transpose(scaled_update, (1, 0, 2)).reshape(rows_here, nblocks * BLOCK)
     new_weight = (weight.astype(jnp.float32) - LEARN_RATE * direction).astype(jnp.bfloat16)
-    new_rows = lax.all_gather(new_weight, "batch", axis=1, tiled=True)
+    ring = [new_weight]
+    for hop in range(3):
+        ring.append(lax.ppermute(ring[-1], "batch", [(dev, (dev + 1) % 4) for dev in range(4)]))
+    new_rows = jnp.roll(
+        jnp.concatenate(ring[::-1], axis=1),
+        (lax.axis_index("batch") + 1) * ring[0].shape[1],
+        axis=1,
+    )
     columns = new_rows
     second_sum = lax.psum_scatter(
         transposed_product(columns, activations).astype(jnp.bfloat16),

time: 725 us -> 670 us (0.924)
  waiting for transfers between devices: 384 us -> 322 us
  local copies, waits for them, and re-layouts: 55.2 us -> 65.9 us
    reduce_scatter x2, waiting for transfers between devices: 151 us -> 71.1 us  [body(): lax.psum_scatter(transposed_product(columns, activations).astype(jnp.bflo...]
    ppermute x0 -> x3, waiting for transfers between devices: none -> 69.2 us  [body(): lax.ppermute(ring[-1], 'batch', [(dev, (dev + 1) % 4) for dev in range(4)])]
    all_gather x1 -> x0, waiting for transfers between devices: 50.5 us -> none  [body(): new_rows = lax.all_gather(new_weight, 'batch', axis=1, tiled=True)]
    unnamed x18 -> x23, local copies, waits for them, and re-layouts: 25.7 us -> 36.2 us
  transfers between devices with their start and end apart: 7 -> 9, of which waited for: 6 -> 7; matrix products, arithmetic and copies ran while one was open for 42% -> 47% of each run, Pallas kernels for 0% -> 0%
where the time goes in v1:
time: 670 us; the launch traced here: 666 us
  waiting for transfers between devices  322 us (48%)
  matrix products  235 us (35%)
  local copies, waits for them, and re-layouts  65.9 us (10%)
  other arithmetic  23.1 us (3%)
  between operations  14.6 us (2%)
    dot_general x11, matrix products, product(): jnp.einsum('bij,bjk->bik', left_mat, right_mat, precision=lax.Precision.H...  180 us
    all_gather x1, waiting for transfers between devices, body(): lax.all_gather(cotangent, ('hidden', 'solver'), axis=0, tiled=True)  77.7 us
    reduce_scatter x2, waiting for transfers between devices, body(): lax.psum_scatter(transposed_product(columns, activations).astype(jnp.bflo...  71.1 us
    reduce_scatter x1, waiting for transfers between devices, body(): lax.psum_scatter(jnp.dot(cotangent_all, activations, preferred_element_ty...  70 us
    ppermute x3, waiting for transfers between devices, body(): lax.ppermute(ring[-1], 'batch', [(dev, (dev + 1) % 4) for dev in range(4)])  69.2 us
    unnamed x23, local copies, waits for them, and re-layouts  36.2 us
    all_gather x1, waiting for transfers between devices, body(): grad_full = lax.all_gather(grad_blocks, 'solver', axis=2, tiled=True)  33.1 us
    dot_general x1, matrix products, body(): jnp.einsum('bnm,bnk->bmk', grad_full, grad_full, preferred_element_type=j...  15.2 us
  transfers between devices with their start and end apart: 9, of which 7 were waited for; matrix products, arithmetic and copies ran while one was open for 47% of the time, Pallas kernels for 0%

profile of v1, /device:TPU:0, one launch (start us, length us, event | category | flops | bytes accessed | tf_op | source)
XLA Modules:
  0.0 666.3 jit_solution(8559374710516171483)
XLA Ops:
  7.2 0.0 all-gather.6.cloned.1.call-start
  7.2 0.7 all-gather.6.cloned.1.call-update
  7.9 0.0 reduce-scatter.6.cloned.1.call-start
  8.0 77.7 %all-gather.6.cloned.1.call-done = bf16[8192,256]{1,0:T(8,128)(2,1)} async-done(((bf16[1024,256]{1,0:T(8,128)(2,1)}), bf16[8192,256]{1,0:T(8,128)(2,1)}) %all-gather.6.cloned.1.call-update) | async-done | bytes 4194320 | tf_op jit(solution)/shard_map/all_gather | solution.py:47
  85.7 7.8 %convolution_convert_fusion = bf16[8192,512]{1,0:T(8,128)(2,1)} fusion(bf16[8192,256]{1,0:T(8,128)(2,1)} %all-gather.6.cloned.1.call-done, bf16[256,512]{1,0:T(8,128)(2,1)S(1)} %copy-done), kind=kOutput, calls=%fused_computation | convolution fusion | flops 2151677952 | bytes 12845056 | tf_op jit(solution)/shard_map/dot_general | solution.py:49
  93.4 0.0 reduce-scatter.6.cloned.1.call-update
  93.5 0.0 all-gather.8.cloned.1.call-start
  93.5 70.0 %reduce-scatter.6.cloned.1.call-done = bf16[2048,512]{1,0:T(8,128)(2,1)} async-done(((bf16[8192,512]{1,0:T(8,128)(2,1)}), bf16[2048,512]{1,0:T(8,128)(2,1)}) %reduce-scatter.6.cloned.1.call-update) | async-done | bytes 2097168 | tf_op jit(solution)/shard_map/reduce_scatter | solution.py:48
  163.5 3.9 copy.32
  167.4 0.0 all-gather.8.cloned.1.call-update
  167.5 0.0 all-gather.4.cloned.1.call-start
  167.5 0.5 all-gather.4.cloned.1.call-update
  168.1 0.2 reduce-scatter.4.cloned.1.call-start
  168.3 2.5 fusion.14
  170.8 2.5 copy.53
  173.3 9.1 %copy.31 = f32[1,2,1024,1024]{2,3,1,0:T(8,128)} copy(f32[1,2,1024,1024]{3,2,1,0:T(8,128)} %param.8) | data formatting | bytes 16777216 | tf_op args[3]
  182.4 8.7 %copy.35 = f32[1,2,1024,1024]{2,3,1,0:T(8,128)} copy(f32[1,2,1024,1024]{3,2,1,0:T(8,128)} %param.9) | data formatting | bytes 16777216 | tf_op args[4]
  191.1 0.2 fusion.18
  191.3 33.1 %all-gather.8.cloned.1.call-done = bf16[2,1024,1024]{1,2,0:T(8,128)(2,1)} async-done(((bf16[2,1024,512]{1,2,0:T(8,128)(2,1)}), bf16[2,1024,1024]{1,2,0:T(8,128)(2,1)}) %all-gather.8.cloned.1.call-update) | async-done | bytes 4194320 | tf_op jit(solution)/shard_map/all_gather | solution.py:57
  224.4 15.2 %abs_reduce_fusion.1 = (f32[2,1024]{1,0:T(2,128)S(1)}, f32[2,1024,1024]{1,2,0:T(8,128)}) fusion(bf16[2,1024,1024]{1,2,0:T(8,128)(2,1)} %all-gather.8.cloned.1.call-done, f32[1,2,1024,1024]{2,3,1,0:T(8,128)} %copy.31), kind=kOutput, calls=%fused_computation.9 | convolution fusion | flops 4305451008 | bytes 20979712 | tf_op jit(solution)/shard_map/bnm,bnk->bmk/dot_general | solution.py:58
  239.6 10.1 %abs_reduce_fusion = (f32[2,1024]{1,0:T(2,128)S(1)}, f32[2,1024,1024]{1,2,0:T(8,128)}) fusion(bf16[2,1024,1024]{1,2,0:T(8,128)(2,1)S(1)} %copy-done.3, f32[1,2,1024,1024]{2,3,1,0:T(8,128)} %copy.35), kind=kOutput, calls=%fused_computation.7 | convolution fusion | flops 4305451008 | bytes 20979712 | tf_op jit(solution)/shard_map/bnm,bkm->bnk/dot_general | solution.py:59
  249.7 0.1 reduce_max.19
  249.8 0.1 reduce_max.18
  249.9 11.4 %subtract_multiply_fusion = (f32[2,1024,1024]{1,2,0:T(8,128)S(1)}, f32[2,1024,1024]{1,2,0:T(8,128)}) fusion(f32[2,1024,1024]{1,2,0:T(8,128)} %get-tuple-element.22, f32[2]{0:T(128)S(1)} %get-tuple-element.16, f32[1024,1024]{0,1:T(8,128)} %fusion.14, f32[2,1024,1024]{1,2,0:T(8,128)} %get-tuple-element.24, f32[2]{0:T(128)S(1)} %get-tuple-element.28), kind=kLoop, calls=%fused_computation.6 | loop fusion | flops 12582912 | bytes 37748752 | tf_op jit(solution)/shard_map/mul | solution.py:26
  261.4 31.4 %fusion.11 = f32[2,512,1024]{2,1,0:T(8,128)S(1)} fusion(f32[2,1024,1024]{1,2,0:T(8,128)} %get-tuple-element.20, s32[]{:T(128)S(6)} %select_n.18), kind=kOutput, calls=%fused_computation.24 | convolution fusion | flops 12884901888 | bytes 16777220 | tf_op jit(solution)/shard_map/bij,bjk->bik/dot_general | solution.py:13
  292.8 14.3 %fusion.24 = f32[2,512,1024]{2,1,0:T(8,128)S(1)} fusion(f32[2,512,1024]{2,1,0:T(8,128)S(1)} %fusion.11, f32[2,1024,1024]{1,2,0:T(8,128)S(1)} %copy-done.1), kind=kOutput, calls=%fused_computation.53 | convolution fusion | flops 12884901888 | bytes 16777216 | tf_op jit(solution)/shard_map/bij,bjk->bik/dot_general | solution.py:13
  307.1 14.3 %fusion.25 = f32[2,512,1024]{2,1,0:T(8,128)S(1)} fusion(f32[2,512,1024]{2,1,0:T(8,128)S(1)} %fusion.24, f32[2,1024,1024]{1,2,0:T(8,128)S(1)} %copy-done.1), kind=kOutput, calls=%fused_computation.54 | convolution fusion | flops 12884901888 | bytes 16777216 | tf_op jit(solution)/shard_map/bij,bjk->bik/dot_general | solution.py:13
  321.4 16.3 %fusion.3 = f32[2,512,1024]{2,1,0:T(8,128)S(1)} fusion(f32[2,512,1024]{2,1,0:T(8,128)S(1)} %fusion.25, f32[2,1024,1024]{1,2,0:T(8,128)} %get-tuple-element.24, f32[2]{0:T(128)S(1)} %get-tuple-element.28), kind=kOutput, calls=%fused_computation.12 | convolution fusion | flops 12886999040 | bytes 16777224 | tf_op jit(solution)/shard_map/bij,bjk->bik/dot_general | solution.py:13
  337.7 15.6 %fusion.8 = f32[2,512,1024]{2,1,0:T(8,128)} fusion(f32[2,1024,1024]{1,2,0:T(8,128)S(1)} %copy-done.1, f32[2,512,1024]{2,1,0:T(8,128)S(1)} %fusion.3, f32[512,1024]{1,0:T(8,128)S(1)} %fusion.18), kind=kOutput, calls=%fused_computation.21 | convolution fusion | flops 12886999040 | bytes 18874368 | tf_op jit(solution)/shard_map/bij,bjk->bik/dot_general | solution.py:13
  353.3 9.4 %fusion.6 = f32[2,512,1024]{2,1,0:T(8,128)S(1)} fusion(bf16[2,1024,1024]{1,2,0:T(8,128)(2,1)} %all-gather.8.cloned.1.call-done, f32[2,512,1024]{2,1,0:T(8,128)} %fusion.8, f32[2]{0:T(128)S(1)} %get-tuple-element.27), kind=kOutput, calls=%fused_computation.19 | convolution fusion | flops 12885950464 | bytes 12582920 | tf_op jit(solution)/shard_map/brm,bnm->brn/dot_general | solution.py:78
  362.7 14.3 %fusion.26 = f32[2,512,1024]{2,1,0:T(8,128)S(1)} fusion(f32[2,512,1024]{2,1,0:T(8,128)S(1)} %fusion.6, f32[2,1024,1024]{1,2,0:T(8,128)S(1)} %get-tuple-element.19), kind=kOutput, calls=%fused_computation.55 | convolution fusion | flops 12884901888 | bytes 16777216 | tf_op jit(solution)/shard_map/bij,bjk->bik/dot_general | solution.py:13
  377.1 14.6 %fusion.27 = f32[2,512,1024]{2,1,0:T(8,128)S(1)} fusion(f32[2,512,1024]{2,1,0:T(8,128)S(1)} %fusion.26, f32[2,1024,1024]{1,2,0:T(8,128)S(1)} %get-tuple-element.19), kind=kOutput, calls=%fused_computation.56 | convolution fusion | flops 12884901888 | bytes 16777216 | tf_op jit(solution)/shard_map/bij,bjk->bik/dot_general | solution.py:13
  391.7 14.3 %fusion.28 = f32[2,512,1024]{2,1,0:T(8,128)S(1)} fusion(f32[2,512,1024]{2,1,0:T(8,128)S(1)} %fusion.27, f32[2,1024,1024]{1,2,0:T(8,128)S(1)} %get-tuple-element.19), kind=kOutput, calls=%fused_computation.57 | convolution fusion | flops 12884901888 | bytes 16777216 | tf_op jit(solution)/shard_map/bij,bjk->bik/dot_general | solution.py:13
  406.0 14.4 %fusion.29 = f32[2,512,1024]{2,1,0:T(8,128)S(1)} fusion(f32[2,512,1024]{2,1,0:T(8,128)S(1)} %fusion.28, f32[2,1024,1024]{1,2,0:T(8,128)S(1)} %get-tuple-element.19), kind=kOutput, calls=%fused_computation.58 | convolution fusion | flops 12884901888 | bytes 16777216 | tf_op jit(solution)/shard_map/bij,bjk->bik/dot_general | solution.py:13
  420.4 14.7 %fusion.30 = f32[2,512,1024]{2,1,0:T(8,128)S(1)} fusion(f32[2,512,1024]{2,1,0:T(8,128)S(1)} %fusion.29, f32[2,1024,1024]{1,2,0:T(8,128)S(1)} %get-tuple-element.19), kind=kOutput, calls=%fused_computation.59 | convolution fusion | flops 12884901888 | bytes 16777216 | tf_op jit(solution)/shard_map/bij,bjk->bik/dot_general | solution.py:13
  435.1 16.0 %multiply_reduce_fusion = (f32[2]{0:T(128)S(1)}, f32[2,512,1024]{2,1,0:T(8,128)}) fusion(f32[2]{0:T(128)S(1)} %get-tuple-element.15, f32[2,512,1024]{2,1,0:T(8,128)S(1)} %fusion.30, f32[2,1024,1024]{1,2,0:T(8,128)S(1)} %bitcast.40, f32[2]{0:T(128)S(1)} %get-tuple-element.16, f32[2,512,1024]{2,1,0:T(8,128)S(1)} %fusion.26), kind=kOutput, calls=%fused_computation.16 | convolution fusion | flops 12892241920 | bytes 20971544 | tf_op jit(solution)/shard_map/bij,bjk->bik/dot_general | solution.py:13
  451.1 4.9 psum.7
  456.0 5.1 divide_bitcast_fusion
  461.1 5.4 copy.52
  466.5 3.5 subtract_convert_fusion
  470.0 0.1 collective-permute-start
  470.1 0.0 all-gather.4.cloned.1.call-done
  470.1 7.7 %convolution_convert_fusion.2 = bf16[8192,256]{1,0:T(8,128)(2,1)} fusion(bf16[512,8192]{1,0:T(8,128)(2,1)} %all-gather.4.cloned.1.call-done, bf16[256,512]{1,0:T(8,128)(2,1)S(1)} %copy-done), kind=kOutput, calls=%fused_computation.2 | convolution fusion | flops 2149580800 | bytes 12845056 | tf_op jit(solution)/shard_map/dot_general | solution.py:31
  477.9 0.0 reduce-scatter.4.cloned.1.call-update
  477.9 0.0 reduce-scatter.8.cloned.1.call-start
  477.9 17.7 %collective-permute-done = bf16[512,2048]{0,1:T(8,128)(2,1)} collective-permute-done((bf16[512,2048]{0,1:T(8,128)(2,1)S(1)}, bf16[512,2048]{0,1:T(8,128)(2,1)}, u32[]{:S(2)}, u32[]{:S(2)}) %collective-permute-start) | collective-permute-done | bytes 2097184 | tf_op jit(solution)/shard_map/ppermute | solution.py:99
  495.7 25.8 %collective-permute-done.1 = bf16[512,2048]{0,1:T(8,128)(2,1)} collective-permute-done((bf16[512,2048]{0,1:T(8,128)(2,1)}, bf16[512,2048]{0,1:T(8,128)(2,1)}, u32[]{:S(2)}, u32[]{:S(2)}) %collective-permute-start.1) | collective-permute-done | bytes 2097184 | tf_op jit(solution)/shard_map/ppermute | solution.py:99
  521.4 0.2 collective-permute-start.2
  521.7 25.7 %collective-permute-done.2 = bf16[512,2048]{0,1:T(8,128)(2,1)} collective-permute-done((bf16[512,2048]{0,1:T(8,128)(2,1)}, bf16[512,2048]{0,1:T(8,128)(2,1)}, u32[]{:S(2)}, u32[]{:S(2)}) %collective-permute-start.2) | collective-permute-done | bytes 2097184 | tf_op jit(solution)/shard_map/ppermute | solution.py:99
  547.4 1.7 constant_dynamic-update-slice_fusion.7
  549.1 1.7 constant_dynamic-update-slice_fusion.6
  550.9 1.7 constant_dynamic-update-slice_fusion.5
  552.6 0.1 constant_dynamic-update-slice_fusion.4
  552.7 1.7 constant_dynamic-update-slice_fusion.3
  554.5 1.7 constant_dynamic-update-slice_fusion.2
  556.2 1.7 constant_dynamic-update-slice_fusion.1
  558.0 0.1 constant_dynamic-update-slice_fusion
  558.1 4.3 convolution_convert_fusion.1
  562.5 4.7 constant_dynamic-slice_fusion.1
  567.1 5.3 copy.34
  572.5 4.6 constant_dynamic-slice_fusion
  577.1 5.7 copy.38
  582.8 5.4 copy.54
  588.2 71.1 %reduce-scatter.8.cloned.1.call-done = bf16[1024,256]{1,0:T(8,128)(2,1)} async-done(((bf16[8192,256]{1,0:T(8,128)(2,1)}), bf16[1024,256]{1,0:T(8,128)(2,1)}) %reduce-scatter.8.cloned.1.call-update) | async-done | bytes 524304 | tf_op jit(solution)/shard_map/reduce_scatter | solution.py:106
  (19 shorter events, 0.1 us)
Async XLA Ops:
  7.2 78.5 %copy-start = (bf16[256,512]{1,0:T(8,128)(2,1)S(1)}, bf16[256,512]{1,0:T(8,128)(2,1)}, u32[]{:S(2)}) copy-start(bf16[256,512]{1,0:T(8,128)(2,1)} %param.5) | copy-start | bytes 786436
  7.2 78.5 %all-gather.6.cloned.1.call-start = ((), (), s32[]{:S(2)}) async-start(), calls=%async_computation.5 | async-start | bytes 4718592 | tf_op jit(solution)/shard_map/all_gather | solution.py:47
  7.9 155.6 %reduce-scatter.6.cloned.1.call-start = ((), (), s32[]{:S(2)}) async-start(), calls=%async_computation.6 | async-start | bytes 10485760 | tf_op jit(solution)/shard_map/reduce_scatter | solution.py:48
  93.5 130.9 %all-gather.8.cloned.1.call-start = ((), (), s32[]{:S(2)}) async-start(), calls=%async_computation.7 | async-start | bytes 6291456 | tf_op jit(solution)/shard_map/all_gather | solution.py:57
  167.4 3.4 copy-start.2
  167.5 302.7 %all-gather.4.cloned.1.call-start = ((), (), s32[]{:S(2)}) async-start(), calls=%async_computation.3 | async-start | bytes 10485760 | tf_op jit(solution)/shard_map/all_gather | solution.py:39
  168.1 420.1 %reduce-scatter.4.cloned.1.call-start = ((), (), s32[]{:S(2)}) async-start(), calls=%async_computation.4 | async-start | bytes 4718592 | tf_op jit(solution)/shard_map/reduce_scatter | solution.py:41
  224.4 15.2 %copy-start.3 = (bf16[2,1024,1024]{1,2,0:T(8,128)(2,1)S(1)}, bf16[2,1024,1024]{1,2,0:T(8,128)(2,1)}, u32[]{:S(2)}) copy-start(bf16[2,1024,1024]{1,2,0:T(8,128)(2,1)} %all-gather.8.cloned.1.call-done) | copy-start | bytes 12582916
  261.4 31.4 %copy-start.1 = (f32[2,1024,1024]{1,2,0:T(8,128)S(1)}, f32[2,1024,1024]{1,2,0:T(8,128)}, u32[]{:S(2)}) copy-start(f32[2,1024,1024]{1,2,0:T(8,128)} %get-tuple-element.20) | copy-start | bytes 25165828
  406.0 29.1 %slice-start = ((s8[8388608]{0:T(1024)(128)(4,1)}), s8[4194304]{0:T(1024)(128)(4,1)S(1)}, s32[]{:S(2)}) async-start(s8[8388608]{0:T(1024)(128)(4,1)} %bitcast.39), calls=%async_computation.9 | async-start | bytes 8388608
  420.4 14.7 %slice-start.1 = ((s8[8388608]{0:T(1024)(128)(4,1)}), s8[4194304]{0:T(1024)(128)(4,1)S(1)}, s32[]{:S(2)}) async-start(s8[8388608]{0:T(1024)(128)(4,1)} %bitcast.39), calls=%async_computation.10 | async-start | bytes 8388608
  470.0 25.6 %collective-permute-start = (bf16[512,2048]{0,1:T(8,128)(2,1)S(1)}, bf16[512,2048]{0,1:T(8,128)(2,1)}, u32[]{:S(2)}, u32[]{:S(2)}) collective-permute-start(bf16[512,2048]{0,1:T(8,128)(2,1)S(1)} %subtract_convert_fusion), channel_id=1, source_target_pairs={{0,8},{8,16},{16,24},{24,0},{1,9},{9,17},{17,25},{25,1},{2,10},{10... | collective-permute-start | bytes 6291464 | tf_op jit(solution)/shard_map/ppermute | solution.py:99
  477.9 181.4 %reduce-scatter.8.cloned.1.call-start = ((), (), s32[]{:S(2)}) async-start(), calls=%async_computation.8 | async-start | bytes 4718592 | tf_op jit(solution)/shard_map/reduce_scatter | solution.py:106
  495.7 25.8 %collective-permute-start.1 = (bf16[512,2048]{0,1:T(8,128)(2,1)}, bf16[512,2048]{0,1:T(8,128)(2,1)}, u32[]{:S(2)}, u32[]{:S(2)}) collective-permute-start(bf16[512,2048]{0,1:T(8,128)(2,1)} %collective-permute-done), channel_id=1, source_target_pairs={{0,8},{8,16},{16,24},{24,0},{1,9},{9,17},{17,25},{25,1},{2,10},{10... | collective-permute-start | bytes 6291464 | tf_op jit(solution)/shard_map/ppermute | solution.py:99
  521.4 26.0 %collective-permute-start.2 = (bf16[512,2048]{0,1:T(8,128)(2,1)}, bf16[512,2048]{0,1:T(8,128)(2,1)}, u32[]{:S(2)}, u32[]{:S(2)}) collective-permute-start(bf16[512,2048]{0,1:T(8,128)(2,1)} %collective-permute-done.1), channel_id=1, source_target_pairs={{0,8},{8,16},{16,24},{24,0},{1,9},{9,17},{17,25},{25,1},{2,10},{10... | collective-permute-start | bytes 6291464 | tf_op jit(solution)/shard_map/ppermute | solution.py:99
Sparse Core Ops, SparseCore 0:
  10.1 75.5 all-gather.5
  93.6 69.8 reduce-scatter.5
  167.6 56.7 all-gather.7
  225.8 58.2 all-gather.3
  478.0 89.1 reduce-scatter.3
  571.3 87.9 reduce-scatter.7
